TPU v7x, 32 devices: a whole 2x2x4 slice. The times are simulated.
32 devices in a mesh: groups: 2 (over y), space: 4 (over x, core), chan: 4 (over z).
Axes of the slice: x: 2, y: 2, z: 4, core: 2. Of those that a mesh axis runs over, the one named last changes fastest.
Arguments:
- fields: bfloat16 [1024, 16, 256], P('chan', ('groups', 'space')), parts along dimension 1, may hold values from -6 to 6
- conv_weight: bfloat16 [27, 1024, 1024], P(None, 'chan', 'space'), may hold values from -0.0390625 to 0.0390625
Outputs:
- convolved: bfloat16 [1024, 16, 256], P('chan', ('groups', 'space')), parts along dimension 1
There are 2 independent parts, one for each index of `groups`. A program takes and returns all parts, laid end to end along the dimension named above; an argument that names none is the same for every part. Nothing has to cross between parts.
All inputs are finite; a program needn't handle non-finite values.
Results may differ from a plain program's by a relative error of at most 0.001.
Values may be sent and summed in bfloat16 or wider, within the bound.
A program may use at most 128 MiB of HBM per device.

v0:
```python
import jax
import jax.numpy as jnp
from jax import lax
from jax.sharding import PartitionSpec as P

NY = 16
NZ = 16


def padded_2(block, sides, width):
    for axis, dim in sides:
        count = lax.axis_size(axis)
        forward = [(i, i + 1) for i in range(count - 1)]
        backward = [(target, source) for source, target in forward]
        low = lax.ppermute(
            lax.slice_in_dim(block, block.shape[dim] - width, None, axis=dim), axis, forward
        )
        high = lax.ppermute(lax.slice_in_dim(block, 0, width, axis=dim), axis, backward)
        block = jnp.concatenate([low, block, high], axis=dim)
    return block


def convolve_block(summed, block, weights):
    count = block.shape[0]
    depth = block.shape[1] - 2
    shaped = block.reshape(count, depth + 2, NY, NZ)
    padded = jnp.pad(shaped, ((0, 0), (0, 0), (1, 1), (1, 1)))
    for step_x in range(3):
        for step_y in range(3):
            for step_z in range(3):
                window = padded[
                    :, step_x : step_x + depth, step_y : step_y + NY, step_z : step_z + NZ
                ].reshape(count, depth * NY * NZ)
                summed = summed + jnp.dot(
                    weights[9 * step_x + 3 * step_y + step_z],
                    window,
                    preferred_element_type=jnp.float32,
                )
    return summed


def local(fields, conv_weight):
    depth = fields.shape[1]
    owned = conv_weight.shape[1]
    weights = lax.all_gather(conv_weight, "space", axis=2, tiled=True)
    empty = jnp.zeros((owned, depth * NY * NZ), jnp.float32)
    gathered = lax.all_gather(fields, "chan", axis=0, tiled=True)
    framed = padded_2(gathered, (("space", 1),), 1)
    summed = convolve_block(empty, framed, weights)
    return summed.reshape(owned, depth, NY * NZ).astype(jnp.bfloat16)


def solution(mesh):
    return jax.shard_map(
        local,
        mesh=mesh,
        in_specs=(P("chan", ("groups", "space"), None), P(None, "chan", "space")),
        out_specs=P("chan", ("groups", "space"), None),
        check_vma=False,
    )
```

profile of v0, /device:TPU:0, one launch (start us, length us, event | category | flops | bytes accessed | tf_op | source)
XLA Modules:
  0.0 168.2 jit_solution(9444668171630820183)
XLA Ops:
  6.5 1.8 %copy.4 = bf16[256,2,256]{0,2,1:T(8,128)(2,1)} copy(bf16[256,2,256]{2,1,0:T(2,128)(2,1)} %param.2) | data formatting | bytes 524288 | tf_op args[0]
  8.4 0.7 all-gather.5.cloned.1.call-update
  9.1 32.5 %all-gather.3.cloned.1.call-done = bf16[1024,2,256]{0,2,1:T(8,128)(2,1)} async-done(((bf16[256,2,256]{0,2,1:T(8,128)(2,1)}), bf16[1024,2,256]{0,2,1:T(8,128)(2,1)}) %all-gather.3.cloned.1.call-update) | async-done | bytes 1048592 | tf_op jit(solution)/shard_map/all_gather | solution.py:47
  41.6 1.3 fusion.13
  42.9 1.3 collective-permute-start.1
  44.1 3.1 %collective-permute-start = (bf16[1024,1,256]{0,2,1:T(8,128)(2,1)S(1)}, bf16[1024,1,256]{0,2,1:T(8,128)(2,1)S(1)}, u32[]{:S(2)}, u32[]{:S(2)}) collective-permute-start(bf16[1024,1,256]{0,2,1:T(8,128)(2,1)S(1)} %get-tuple-element.32), channel_id=1, source_target_pairs={{0,4},{4,8},{8,12},{1,5},{5,9},{9,13},{2,6},{6,10},{10,14},{3,7},{... | collective-permute-start | bytes 1572872 | tf_op jit(solution)/shard_map/ppermute | solution.py:15
  47.2 1.5 collective-permute-done
  48.7 1.6 pad_maximum_fusion
  50.3 3.4 %pad_slice_fusion.1 = (bf16[1024,2,16,16]{0,3,2,1:T(8,128)(2,1)S(1)}, bf16[1024,2,16,16]{0,3,2,1:T(8,128)(2,1)}, bf16[1024,2,16,16]{0,3,2,1:T(8,128)(2,1)S(1)}, ...) fusion(bf16[1024,4,16,16]{0,3,2,1:T(8,128)(2,1)S(1)} %bitcast.181), kind=kLoop, calls=%fused_computation.1 | loop fusion | bytes 13631488 | tf_op jit(solution)/shard_map/slice | solution.py:31
  53.7 7.4 %pad_slice_fusion = (bf16[1024,2,16,16]{0,3,2,1:T(8,128)(2,1)}, bf16[1024,2,16,16]{0,3,2,1:T(8,128)(2,1)}, bf16[1024,2,16,16]{0,3,2,1:T(8,128)(2,1)}, bf16[1024,...) fusion(bf16[1024,4,16,16]{0,3,2,1:T(8,128)(2,1)S(1)} %bitcast.182), kind=kLoop, calls=%fused_computation | loop fusion | bytes 22020096 | tf_op jit(solution)/shard_map/slice | solution.py:31
  61.1 73.3 %all-gather.5.cloned.1.call-done = bf16[27,256,1024]{2,1,0:T(8,128)(2,1)} async-done(((bf16[27,256,256]{2,1,0:T(8,128)(2,1)}), bf16[27,256,1024]{2,1,0:T(8,128)(2,1)}) %all-gather.5.cloned.1.call-update) | async-done | bytes 14155792 | tf_op jit(solution)/shard_map/all_gather | solution.py:45
  134.4 2.0 %convolution_bitcast_fusion.8 = f32[256,512]{0,1:T(8,128)S(1)} fusion(bf16[1024,512]{0,1:T(8,128)(2,1)} %bitcast.210, bf16[27,256,1024]{2,1,0:T(8,128)(2,1)} %all-gather.5.cloned.1.call-done), kind=kOutput, calls=%fused_computation.59 | convolution fusion | flops 268435456 | bytes 2097152 | tf_op jit(solution)/shard_map/dot_general | solution.py:34
  136.4 2.6 %convolution_bitcast_fusion.9 = f32[256,512]{0,1:T(8,128)S(1)} fusion(bf16[1024,512]{0,1:T(8,128)(2,1)} %bitcast.209, bf16[27,256,1024]{2,1,0:T(8,128)(2,1)} %all-gather.5.cloned.1.call-done), kind=kOutput, calls=%fused_computation.60 | convolution fusion | flops 268435456 | bytes 2097152 | tf_op jit(solution)/shard_map/dot_general | solution.py:34
  139.0 2.6 %fusion.12 = f32[512,256]{1,0:T(8,128)S(1)} fusion(bf16[1024,512]{0,1:T(8,128)(2,1)} %bitcast.208, bf16[27,256,1024]{2,1,0:T(8,128)(2,1)} %all-gather.5.cloned.1.call-done), kind=kOutput, calls=%fused_computation.89 | convolution fusion | flops 268435456 | bytes 2097152 | tf_op jit(solution)/shard_map/dot_general | solution.py:34
  141.6 1.9 %convolution_add_fusion.15 = f32[512,256]{1,0:T(8,128)S(1)} fusion(f32[512,256]{1,0:T(8,128)S(1)} %fusion.12, bf16[1024,512]{0,1:T(8,128)(2,1)} %bitcast.190, bf16[27,256,1024]{2,1,0:T(8,128)(2,1)} %all-gather.5.cloned.1.call-done), kind=kOutput, calls=%fused_computation.41 | convolution fusion | flops 268566528 | bytes 2621440 | tf_op jit(solution)/shard_map/dot_general | solution.py:34
  143.6 1.9 %convolution_add_fusion.14 = f32[512,256]{1,0:T(8,128)S(1)} fusion(f32[512,256]{1,0:T(8,128)S(1)} %convolution_add_fusion.15, bf16[1024,512]{0,1:T(8,128)(2,1)} %bitcast.206, bf16[27,256,1024]{2,1,0:T(8,128)(2,1)} %all-gather.5.cloned.1.call-done), kind=kOutput, calls=%fused_computation.40 | convolution fusion | flops 268566528 | bytes 2621440 | tf_op jit(solution)/shard_map/dot_general | solution.py:34
  145.5 1.9 %convolution_add_fusion.13 = f32[512,256]{1,0:T(8,128)S(1)} fusion(f32[512,256]{1,0:T(8,128)S(1)} %convolution_add_fusion.14, bf16[1024,512]{0,1:T(8,128)(2,1)} %bitcast.205, bf16[27,256,1024]{2,1,0:T(8,128)(2,1)} %all-gather.5.cloned.1.call-done), kind=kOutput, calls=%fused_computation.39 | convolution fusion | flops 268566528 | bytes 2621440 | tf_op jit(solution)/shard_map/dot_general | solution.py:34
  147.5 1.8 %convolution_add_fusion.12 = f32[512,256]{1,0:T(8,128)S(1)} fusion(f32[512,256]{1,0:T(8,128)S(1)} %convolution_add_fusion.13, bf16[1024,512]{0,1:T(8,128)(2,1)} %bitcast.189, bf16[27,256,1024]{2,1,0:T(8,128)(2,1)S(1)} %copy-done), kind=kOutput, calls=%fused_computation.38 | convolution fusion | flops 268566528 | bytes 2621440 | tf_op jit(solution)/shard_map/dot_general | solution.py:34
  149.3 1.8 %convolution_add_fusion.11 = f32[512,256]{1,0:T(8,128)S(1)} fusion(f32[512,256]{1,0:T(8,128)S(1)} %convolution_add_fusion.12, bf16[1024,512]{0,1:T(8,128)(2,1)} %bitcast.204, bf16[27,256,1024]{2,1,0:T(8,128)(2,1)S(1)} %copy-done), kind=kOutput, calls=%fused_computation.37 | convolution fusion | flops 268566528 | bytes 2621440 | tf_op jit(solution)/shard_map/dot_general | solution.py:34
  151.1 0.5 convolution_add_fusion.10
  152.1 0.5 convolution_add_fusion.8
  152.6 0.5 convolution_add_fusion.7
  153.1 0.5 convolution_add_fusion.6
  153.6 0.5 convolution_add_fusion.5
  154.6 0.5 convolution_add_fusion.3
  155.1 0.5 convolution_add_fusion.2
  157.1 0.5 fusion.8
  158.1 0.5 fusion.6
  159.0 0.5 fusion.4
  159.5 0.5 fusion.3
  160.0 0.5 fusion.11
  160.5 0.9 copy.5
  (45 shorter events, 3.5 us)
Async XLA Ops:
  6.5 35.0 %all-gather.3.cloned.1.call-start = ((), (), s32[]{:S(2)}) async-start(), calls=%async_computation | async-start | bytes 1310720 | tf_op jit(solution)/shard_map/all_gather | solution.py:47
  8.4 126.0 %all-gather.5.cloned.1.call-start = ((), (), s32[]{:S(2)}) async-start(), calls=%async_computation.1 | async-start | bytes 17694720 | tf_op jit(solution)/shard_map/all_gather | solution.py:45
  42.9 4.4 %collective-permute-start.1 = (bf16[1024,1,256]{0,2,1:T(8,128)(2,1)S(1)}, bf16[1024,1,256]{0,2,1:T(8,128)(2,1)S(1)}, u32[]{:S(2)}, u32[]{:S(2)}) collective-permute-start(bf16[1024,1,256]{0,2,1:T(8,128)(2,1)S(1)} %get-tuple-element.33), channel_id=1, source_target_pairs={{4,0},{8,4},{12,8},{5,1},{9,5},{13,9},{6,2},{10,6},{14,10},{7,3},{... | collective-permute-start | bytes 1572872 | tf_op jit(solution)/shard_map/ppermute | solution.py:18
  44.1 4.6 %collective-permute-start = (bf16[1024,1,256]{0,2,1:T(8,128)(2,1)S(1)}, bf16[1024,1,256]{0,2,1:T(8,128)(2,1)S(1)}, u32[]{:S(2)}, u32[]{:S(2)}) collective-permute-start(bf16[1024,1,256]{0,2,1:T(8,128)(2,1)S(1)} %get-tuple-element.32), channel_id=1, source_target_pairs={{0,4},{4,8},{8,12},{1,5},{5,9},{9,13},{2,6},{6,10},{10,14},{3,7},{... | collective-permute-start | bytes 1572872 | tf_op jit(solution)/shard_map/ppermute | solution.py:15
  134.4 13.1 %copy-start = (bf16[27,256,1024]{2,1,0:T(8,128)(2,1)S(1)}, bf16[27,256,1024]{2,1,0:T(8,128)(2,1)}, u32[]{:S(2)}) copy-start(bf16[27,256,1024]{2,1,0:T(8,128)(2,1)} %all-gather.5.cloned.1.call-done) | copy-start | bytes 42467332
  134.4 16.7 %copy-start.16 = (bf16[1024,2,16,16]{0,3,2,1:T(8,128)(2,1)S(1)}, bf16[1024,2,16,16]{0,3,2,1:T(8,128)(2,1)}, u32[]{:S(2)}) copy-start(bf16[1024,2,16,16]{0,3,2,1:T(8,128)(2,1)} %get-tuple-element.10) | copy-start | bytes 3145732
  134.4 17.2 %copy-start.15 = (bf16[1024,2,16,16]{0,3,2,1:T(8,128)(2,1)S(1)}, bf16[1024,2,16,16]{0,3,2,1:T(8,128)(2,1)}, u32[]{:S(2)}) copy-start(bf16[1024,2,16,16]{0,3,2,1:T(8,128)(2,1)} %get-tuple-element.11) | copy-start | bytes 3145732
  134.4 17.7 %copy-start.14 = (bf16[1024,2,16,16]{0,3,2,1:T(8,128)(2,1)S(1)}, bf16[1024,2,16,16]{0,3,2,1:T(8,128)(2,1)}, u32[]{:S(2)}) copy-start(bf16[1024,2,16,16]{0,3,2,1:T(8,128)(2,1)} %get-tuple-element.12) | copy-start | bytes 3145732
  134.4 18.2 %copy-start.13 = (bf16[1024,2,16,16]{0,3,2,1:T(8,128)(2,1)S(1)}, bf16[1024,2,16,16]{0,3,2,1:T(8,128)(2,1)}, u32[]{:S(2)}) copy-start(bf16[1024,2,16,16]{0,3,2,1:T(8,128)(2,1)} %get-tuple-element.13) | copy-start | bytes 3145732
  136.4 16.7 %copy-start.12 = (bf16[1024,2,16,16]{0,3,2,1:T(8,128)(2,1)S(1)}, bf16[1024,2,16,16]{0,3,2,1:T(8,128)(2,1)}, u32[]{:S(2)}) copy-start(bf16[1024,2,16,16]{0,3,2,1:T(8,128)(2,1)} %get-tuple-element.14) | copy-start | bytes 3145732
  139.0 14.6 %copy-start.11 = (bf16[1024,2,16,16]{0,3,2,1:T(8,128)(2,1)S(1)}, bf16[1024,2,16,16]{0,3,2,1:T(8,128)(2,1)}, u32[]{:S(2)}) copy-start(bf16[1024,2,16,16]{0,3,2,1:T(8,128)(2,1)} %get-tuple-element.15) | copy-start | bytes 3145732
  141.6 12.4 %copy-start.10 = (bf16[1024,2,16,16]{0,3,2,1:T(8,128)(2,1)S(1)}, bf16[1024,2,16,16]{0,3,2,1:T(8,128)(2,1)}, u32[]{:S(2)}) copy-start(bf16[1024,2,16,16]{0,3,2,1:T(8,128)(2,1)} %get-tuple-element.16) | copy-start | bytes 3145732
  143.6 11.0 %copy-start.3 = (bf16[1024,2,16,16]{0,3,2,1:T(8,128)(2,1)S(1)}, bf16[1024,2,16,16]{0,3,2,1:T(8,128)(2,1)}, u32[]{:S(2)}) copy-start(bf16[1024,2,16,16]{0,3,2,1:T(8,128)(2,1)} %get-tuple-element.29) | copy-start | bytes 3145732
  145.5 9.6 %copy-start.9 = (bf16[1024,2,16,16]{0,3,2,1:T(8,128)(2,1)S(1)}, bf16[1024,2,16,16]{0,3,2,1:T(8,128)(2,1)}, u32[]{:S(2)}) copy-start(bf16[1024,2,16,16]{0,3,2,1:T(8,128)(2,1)} %get-tuple-element.17) | copy-start | bytes 3145732
  147.5 8.1 %copy-start.8 = (bf16[1024,2,16,16]{0,3,2,1:T(8,128)(2,1)S(1)}, bf16[1024,2,16,16]{0,3,2,1:T(8,128)(2,1)}, u32[]{:S(2)}) copy-start(bf16[1024,2,16,16]{0,3,2,1:T(8,128)(2,1)} %get-tuple-element.18) | copy-start | bytes 3145732
  149.3 6.8 %copy-start.4 = (bf16[1024,2,16,16]{0,3,2,1:T(8,128)(2,1)S(1)}, bf16[1024,2,16,16]{0,3,2,1:T(8,128)(2,1)}, u32[]{:S(2)}) copy-start(bf16[1024,2,16,16]{0,3,2,1:T(8,128)(2,1)} %get-tuple-element.19) | copy-start | bytes 3145732
  151.6 5.0 %copy-start.7 = (bf16[1024,2,16,16]{0,3,2,1:T(8,128)(2,1)S(1)}, bf16[1024,2,16,16]{0,3,2,1:T(8,128)(2,1)}, u32[]{:S(2)}) copy-start(bf16[1024,2,16,16]{0,3,2,1:T(8,128)(2,1)} %get-tuple-element.22) | copy-start | bytes 3145732
  152.1 5.0 %copy-start.6 = (bf16[1024,2,16,16]{0,3,2,1:T(8,128)(2,1)S(1)}, bf16[1024,2,16,16]{0,3,2,1:T(8,128)(2,1)}, u32[]{:S(2)}) copy-start(bf16[1024,2,16,16]{0,3,2,1:T(8,128)(2,1)} %get-tuple-element.23) | copy-start | bytes 3145732
  152.6 5.0 %copy-start.2 = (bf16[1024,2,16,16]{0,3,2,1:T(8,128)(2,1)S(1)}, bf16[1024,2,16,16]{0,3,2,1:T(8,128)(2,1)}, u32[]{:S(2)}) copy-start(bf16[1024,2,16,16]{0,3,2,1:T(8,128)(2,1)} %get-tuple-element.25) | copy-start | bytes 3145732
  153.1 5.0 %copy-start.1 = (bf16[1024,2,16,16]{0,3,2,1:T(8,128)(2,1)S(1)}, bf16[1024,2,16,16]{0,3,2,1:T(8,128)(2,1)}, u32[]{:S(2)}) copy-start(bf16[1024,2,16,16]{0,3,2,1:T(8,128)(2,1)} %get-tuple-element.28) | copy-start | bytes 3145732
  155.1 4.9 %copy-start.5 = (bf16[1024,2,16,16]{0,3,2,1:T(8,128)(2,1)S(1)}, bf16[1024,2,16,16]{0,3,2,1:T(8,128)(2,1)}, u32[]{:S(2)}) copy-start(bf16[1024,2,16,16]{0,3,2,1:T(8,128)(2,1)} %get-tuple-element.5) | copy-start | bytes 3145732
Sparse Core Ops, SparseCore 0:
  8.9 32.6 all-gather.2
  43.1 91.1 all-gather.4
where the time goes:
time: 169 us; the launch traced here: 168 us
  waiting for transfers between devices  108 us (64%)
  matrix products  25.6 us (15%)
  local copies, waits for them, and re-layouts  14.8 us (9%)
  between operations  13.9 us (8%)
  starting transfers between devices  4.4 us (3%)
    all_gather x1, waiting for transfers between devices, local(): weights = lax.all_gather(conv_weight, 'space', axis=2, tiled=True)  73.3 us
    all_gather x1, waiting for transfers between devices, local(): gathered = lax.all_gather(fields, 'chan', axis=0, tiled=True)  32.5 us
    dot_general x27, matrix products, convolve_block(): jnp.dot(weights[9 * step_x + 3 * step_y + step_z], window, preferred_elem...  25.6 us
    slice x2, local copies, waits for them, and re-layouts, convolve_block(): padded[:, step_x:step_x + depth, step_y:step_y + NY, step_z:step_z + NZ]  10.8 us
  transfers between devices with their start and end apart: 4, of which 3 were waited for; matrix products, arithmetic and copies ran while one was open for 8% of the time, Pallas kernels for 0%

commit v1 on v0

--- a/solution.py
+++ b/solution.py
@@ -42,7 +42,7 @@
 def local(fields, conv_weight):
     depth = fields.shape[1]
     owned = conv_weight.shape[1]
-    weights = lax.all_gather(conv_weight, "space", axis=2, tiled=True)
+    weights = jnp.concatenate(lax.all_gather(conv_weight, "space"), axis=2)
     empty = jnp.zeros((owned, depth * NY * NZ), jnp.float32)
     gathered = lax.all_gather(fields, "chan", axis=0, tiled=True)
     framed = padded_2(gathered, (("space", 1),), 1)

time: 169 us -> 228 us (1.35)
  local copies, waits for them, and re-layouts: 14.8 us -> 83.5 us
  matrix products: 25.6 us -> 15.2 us
    slice x0 -> x29, local copies, waits for them, and re-layouts: none -> 66.9 us  [convolve_block(): weights[9 * step_x + 3 * step_y + step_z]]
    dot_general x27, matrix products: 25.6 us -> 15.2 us  [convolve_block(): jnp.dot(weights[9 * step_x + 3 * step_y + step_z], window, preferred_elem...]
    ppermute x1, waiting for transfers between devices: 0.01 us -> 3.21 us  [padded_2(): lax.ppermute(lax.slice_in_dim(block, 0, width, axis=dim), axis, backward)]
  transfers between devices with their start and end apart: 4 -> 4, of which waited for: 3 -> 4; matrix products, arithmetic and copies ran while one was open for 8% -> 6% of each run, Pallas kernels for 0% -> 0%
where the time goes in v1:
time: 228 us; the launch traced here: 226 us
  waiting for transfers between devices  109 us (48%)
  local copies, waits for them, and re-layouts  83.5 us (37%)
  matrix products  15.2 us (7%)
  between operations  14.2 us (6%)
  starting transfers between devices  2.66 us (1%)
    all_gather x1, waiting for transfers between devices, local(): weights = jnp.concatenate(lax.all_gather(conv_weight, 'space'), axis=2)  72.3 us
    slice x29, local copies, waits for them, and re-layouts, convolve_block(): weights[9 * step_x + 3 * step_y + step_z]  66.9 us
    all_gather x1, waiting for transfers between devices, local(): gathered = lax.all_gather(fields, 'chan', axis=0, tiled=True)  32.5 us
    dot_general x27, matrix products, convolve_block(): jnp.dot(weights[9 * step_x + 3 * step_y + step_z], window, preferred_elem...  15.2 us
    slice x2, local copies, waits for them, and re-layouts, convolve_block(): padded[:, step_x:step_x + depth, step_y:step_y + NY, step_z:step_z + NZ]  11.4 us
  transfers between devices with their start and end apart: 4, of which 4 were waited for; matrix products, arithmetic and copies ran while one was open for 6% of the time, Pallas kernels for 0%

profile of v1, /device:TPU:0, one launch (start us, length us, event | category | flops | bytes accessed | tf_op | source)
XLA Modules:
  0.0 225.9 jit_solution(15484407728358232687)
XLA Ops:
  9.1 32.5 %all-gather.4.cloned.1.call-done = bf16[1024,2,256]{0,2,1:T(8,128)(2,1)} async-done(((bf16[256,2,256]{0,2,1:T(8,128)(2,1)}), bf16[1024,2,256]{0,2,1:T(8,128)(2,1)}) %all-gather.4.cloned.1.call-update) | async-done | bytes 1048592 | tf_op jit(solution)/shard_map/all_gather | solution.py:47
  45.7 3.2 %collective-permute-done.1 = bf16[1024,1,256]{0,2,1:T(8,128)(2,1)S(1)} collective-permute-done((bf16[1024,1,256]{0,2,1:T(8,128)(2,1)S(1)}, bf16[1024,1,256]{0,2,1:T(8,128)(2,1)S(1)}, u32[]{:S(2)}, u32[]{:S(2)}) %collective-permute-start.1) | collective-permute-done | bytes 524320 | tf_op jit(solution)/shard_map/ppermute | solution.py:18
  50.5 3.0 %pad_slice_fusion.1 = (bf16[1024,2,16,16]{0,3,2,1:T(8,128)(2,1)S(1)}, bf16[1024,2,16,16]{0,3,2,1:T(8,128)(2,1)}, bf16[1024,2,16,16]{0,3,2,1:T(8,128)(2,1)S(1)}, ...) fusion(bf16[1024,4,16,16]{0,3,2,1:T(8,128)(2,1)S(1)} %bitcast.157), kind=kLoop, calls=%fused_computation.1 | loop fusion | bytes 13631488 | tf_op jit(solution)/shard_map/slice | solution.py:31
  53.6 8.3 %pad_slice_fusion = (bf16[1024,2,16,16]{0,3,2,1:T(8,128)(2,1)}, bf16[1024,2,16,16]{0,3,2,1:T(8,128)(2,1)}, bf16[1024,2,16,16]{0,3,2,1:T(8,128)(2,1)}, bf16[1024,...) fusion(bf16[1024,4,16,16]{0,3,2,1:T(8,128)(2,1)S(1)} %bitcast.158), kind=kLoop, calls=%fused_computation | loop fusion | bytes 22020096 | tf_op jit(solution)/shard_map/slice | solution.py:31
  61.9 72.3 %all-gather.6.cloned.1.call-done = bf16[108,256,256]{2,1,0:T(8,128)(2,1)} async-done(((bf16[27,256,256]{2,1,0:T(8,128)(2,1)}), bf16[108,256,256]{2,1,0:T(8,128)(2,1)}) %all-gather.6.cloned.1.call-update) | async-done | bytes 14155792 | tf_op jit(solution)/shard_map/all_gather | solution.py:45
  134.1 4.2 %fusion.13 = (bf16[1,256,4,256]{3,1,0,2:T(8,128)(2,1)}, bf16[1,256,4,256]{3,1,0,2:T(8,128)(2,1)}, bf16[1,256,4,256]{3,1,0,2:T(8,128)(2,1)}, bf16[1,256,4,256]{3,...) fusion(bf16[27,256,4,256]{3,1,0,2:T(8,128)(2,1)} %bitcast.159), kind=kLoop, calls=%fused_computation.64 | loop fusion | bytes 8388608 | tf_op jit(solution)/shard_map/slice | solution.py:35
  138.3 7.4 %fusion.12 = (bf16[1,256,4,256]{3,1,0,2:T(8,128)(2,1)}, bf16[1,256,4,256]{3,1,0,2:T(8,128)(2,1)}, bf16[1,256,4,256]{3,1,0,2:T(8,128)(2,1)}, bf16[1,256,4,256]{3,...) fusion(bf16[27,256,4,256]{3,1,0,2:T(8,128)(2,1)} %bitcast.160), kind=kLoop, calls=%fused_computation.63 | loop fusion | bytes 19922944 | tf_op jit(solution)/shard_map/slice | solution.py:35
  145.7 2.1 copy.62
  147.7 2.0 copy.43
  149.8 2.0 copy.42
  151.8 2.0 copy.41
  153.9 2.1 copy.40
  158.0 2.1 copy.38
  160.1 2.0 copy.37
  162.1 2.1 copy.36
  164.2 2.0 copy.61
  166.2 2.0 copy.60
  168.2 2.0 copy.59
  170.3 2.0 copy.58
  174.4 2.0 copy.56
  176.4 2.0 copy.55
  178.5 2.0 copy.54
  180.5 2.0 copy.53
  182.6 2.0 copy.52
  184.6 2.1 copy.51
  186.7 2.0 copy.50
  188.8 2.1 copy.49
  190.8 2.0 copy.48
  192.9 2.0 copy.47
  194.9 2.1 copy.46
  197.0 2.1 copy.45
  199.1 2.1 copy.44
  (134 shorter events, 29.6 us)
Async XLA Ops:
  6.5 35.0 %all-gather.4.cloned.1.call-start = ((), (), s32[]{:S(2)}) async-start(), calls=%async_computation | async-start | bytes 1310720 | tf_op jit(solution)/shard_map/all_gather | solution.py:47
  8.4 125.8 %all-gather.6.cloned.1.call-start = ((), (), s32[]{:S(2)}) async-start(), calls=%async_computation.1 | async-start | bytes 17694720 | tf_op jit(solution)/shard_map/all_gather | solution.py:45
  42.9 2.8 %collective-permute-start = (bf16[1024,1,256]{0,2,1:T(8,128)(2,1)S(1)}, bf16[1024,1,256]{0,2,1:T(8,128)(2,1)S(1)}, u32[]{:S(2)}, u32[]{:S(2)}) collective-permute-start(bf16[1024,1,256]{0,2,1:T(8,128)(2,1)S(1)} %get-tuple-element.59), channel_id=1, source_target_pairs={{0,4},{4,8},{8,12},{1,5},{5,9},{9,13},{2,6},{6,10},{10,14},{3,7},{... | collective-permute-start | bytes 1572872 | tf_op jit(solution)/shard_map/ppermute | solution.py:15
  44.2 4.7 %collective-permute-start.1 = (bf16[1024,1,256]{0,2,1:T(8,128)(2,1)S(1)}, bf16[1024,1,256]{0,2,1:T(8,128)(2,1)S(1)}, u32[]{:S(2)}, u32[]{:S(2)}) collective-permute-start(bf16[1024,1,256]{0,2,1:T(8,128)(2,1)S(1)} %get-tuple-element.60), channel_id=1, source_target_pairs={{4,0},{8,4},{12,8},{5,1},{9,5},{13,9},{6,2},{10,6},{14,10},{7,3},{... | collective-permute-start | bytes 1572872 | tf_op jit(solution)/shard_map/ppermute | solution.py:18
  201.1 3.9 %copy-start.21 = (bf16[1024,2,16,16]{0,3,2,1:T(8,128)(2,1)S(1)}, bf16[1024,2,16,16]{0,3,2,1:T(8,128)(2,1)}, u32[]{:S(2)}) copy-start(bf16[1024,2,16,16]{0,3,2,1:T(8,128)(2,1)} %get-tuple-element.33) | copy-start | bytes 3145732
  201.1 3.9 %copy-start.46 = (bf16[1,256,4,256]{1,3,2,0:T(8,128)(2,1)S(1)}, bf16[1,256,4,256]{1,3,2,0:T(8,128)(2,1)}, u32[]{:S(2)}) copy-start(bf16[1,256,4,256]{1,3,2,0:T(8,128)(2,1)} %copy.37) | copy-start | bytes 1572868
  201.1 4.4 %copy-start.4 = (bf16[1024,2,16,16]{0,3,2,1:T(8,128)(2,1)S(1)}, bf16[1024,2,16,16]{0,3,2,1:T(8,128)(2,1)}, u32[]{:S(2)}) copy-start(bf16[1024,2,16,16]{0,3,2,1:T(8,128)(2,1)} %get-tuple-element.58) | copy-start | bytes 3145732
  201.1 4.4 %copy-start.42 = (bf16[1,256,4,256]{1,3,2,0:T(8,128)(2,1)S(1)}, bf16[1,256,4,256]{1,3,2,0:T(8,128)(2,1)}, u32[]{:S(2)}) copy-start(bf16[1,256,4,256]{1,3,2,0:T(8,128)(2,1)} %copy.36) | copy-start | bytes 1572868
  203.1 2.9 %copy-start.20 = (bf16[1024,2,16,16]{0,3,2,1:T(8,128)(2,1)S(1)}, bf16[1024,2,16,16]{0,3,2,1:T(8,128)(2,1)}, u32[]{:S(2)}) copy-start(bf16[1024,2,16,16]{0,3,2,1:T(8,128)(2,1)} %get-tuple-element.34) | copy-start | bytes 3145732
  203.1 2.9 %copy-start.40 = (bf16[1,256,4,256]{1,3,2,0:T(8,128)(2,1)S(1)}, bf16[1,256,4,256]{1,3,2,0:T(8,128)(2,1)}, u32[]{:S(2)}) copy-start(bf16[1,256,4,256]{1,3,2,0:T(8,128)(2,1)} %copy.38) | copy-start | bytes 1572868
  206.0 1.5 copy-start.34
  206.5 1.5 copy-start.32
  207.0 1.5 copy-start.30
  207.6 1.6 copy-start.44
  208.0 1.5 copy-start.14
  208.1 1.5 copy-start.43
  208.5 1.5 copy-start.41
  209.1 1.6 copy-start.39
  209.6 1.6 copy-start.11
  209.6 1.6 copy-start.37
  210.1 1.6 copy-start.2
  210.1 1.6 copy-start.35
  210.7 1.6 copy-start.33
  211.2 1.6 copy-start.9
  211.2 1.6 copy-start.31
  211.7 1.6 copy-start.5
  211.7 1.6 copy-start.29
  213.7 1.7 copy-start.1
  213.7 1.7 copy-start.26
  214.2 1.6 copy-start
  214.2 1.6 copy-start.25
  214.7 1.6 copy-start.24
  (19 other events, 27.6 us)
Sparse Core Ops, SparseCore 0:
  8.9 32.6 all-gather.3
  43.1 90.9 all-gather.5
